TPU v7x, 256 devices: a whole 4x4x8 slice. The times are simulated.
256 devices in a mesh: seq: 16 (over x_hi, y, core), heads: 16 (over z, x_lo).
Axes of the slice: x: 4 (x_hi: 2, x_lo: 2; x = x_hi * 2 + x_lo), y: 4, z: 8, core: 2. Of those that a mesh axis runs over, the one named last changes fastest.
Arguments:
- activations: bfloat16 [12288, 4096], P('seq', 'heads'), may hold values from -24 to 24
- w_query: bfloat16 [4096, 4096], P(None, 'heads'), may hold values from -0.1875 to 0.1875
- w_key: bfloat16 [4096, 4096], P(None, 'heads'), may hold values from -0.09375 to 0.09375
- w_value: bfloat16 [4096, 4096], P(None, 'heads'), may hold values from -0.09375 to 0.09375
- w_out: bfloat16 [4096, 4096], P('heads'), may hold values from -0.1875 to 0.1875
- windows: int32 [32], P('heads'), may hold values from 1 to 2, as said below
- rand_blocks: int32 [96, 3], P('seq'), may hold values from 0 to 95, as said below
- global_pos: int32 [128], replicated, may hold values from 0 to 12287, as said below
Outputs:
- attended: bfloat16 [12288, 4096], P('seq', 'heads')
Inputs may be any that keep to these rules, and one draw needn't show every extreme that they name: `windows`: some head has reach 2. `rand_blocks`: the 3 entries of a row are distinct. Of the 18 entries in the rows of one index of seq, at most 2 fall into the 6 blocks of any one index, and exactly 2 into those of some index. `global_pos`: Distinct. At most 32 fall into the 768 positions of one index of seq, and exactly 32 into those of some index.
All inputs are finite; a program needn't handle non-finite values.
Results may differ from a plain program's by a relative error of at most 0.024.
The roundings to bfloat16 on the way count: a program that leaves them out, or rounds other values in their place, can miss the bound.
Values may be sent and summed in bfloat16 or wider, within the bound.
No kernel may reach another device: no remote copies, remote signals or barrier semaphores. Data moves between devices by JAX's collectives and lax.ppermute only.
A program may use at most 128 MiB of HBM per device.

v0:
```python
import math

import jax
import jax.numpy as jnp
from jax import lax
from jax.sharding import PartitionSpec as P

WMAX = 2


NEGATIVE = -1e30


def extended(block, sides, width):
    for axis, dim in sides:
        count = lax.axis_size(axis)
        forward = [(i, i + 1) for i in range(count - 1)]
        forward.append((count - 1, 0))
        backward = [(target, source) for source, target in forward]
        low = lax.ppermute(
            lax.slice_in_dim(block, block.shape[dim] - width, None, axis=dim), axis, forward
        )
        high = lax.ppermute(lax.slice_in_dim(block, 0, width, axis=dim), axis, backward)
        block = jnp.concatenate([low, block, high], axis=dim)
    return block


def combined_all(value, axis, join):
    pieces = jax.tree.map(lambda part: lax.all_gather(part, axis), value)
    head = jax.tree.map(lambda part: part[0], pieces)
    tail = jax.tree.map(lambda part: part[1:], pieces)
    running, _ = lax.scan(lambda running, slab: (join(running, slab), None), head, tail)
    return running


def fold_scores(state, scores, valid):
    top_old, sum_old, acc_old = state
    masked = jnp.where(valid, scores, NEGATIVE)
    top_new = jnp.maximum(top_old, jnp.max(masked, axis=-1))
    probs = jnp.where(valid, jnp.exp(masked - top_new[..., None]), 0.0)
    keep = jnp.exp(top_old - top_new)
    return (
        top_new,
        keep * sum_old + jnp.sum(probs, axis=-1),
        keep[..., None] * acc_old,
        probs.astype(jnp.bfloat16),
    )


def join_states(first, second):
    top_first, sum_first, acc_first = first
    top_second, sum_second, acc_second = second
    top_both = jnp.maximum(top_first, top_second)
    keep_first = jnp.exp(top_first - top_both)
    keep_second = jnp.exp(top_second - top_both)
    return (
        top_both,
        keep_first * sum_first + keep_second * sum_second,
        keep_first[..., None] * acc_first + keep_second[..., None] * acc_second,
    )


def on_device(activations, w_query, w_key, w_value, w_out, windows, rand_blocks, global_pos):
    rows_here = activations.shape[0]
    group_width = w_query.shape[1]
    heads_here = windows.shape[0]
    head_size = group_width // heads_here
    blocks_here = rand_blocks.shape[0]
    block_rows = rows_here // blocks_here
    picks_per_block = rand_blocks.shape[1]
    seq_count = lax.axis_size("seq")
    position = lax.axis_index("seq")
    score_scale = 1.0 / math.sqrt(head_size)
    piece = lax.all_gather(activations, "heads", axis=1, tiled=True)
    sums_query = jnp.dot(piece, w_query, preferred_element_type=jnp.float32)
    sums_key = jnp.dot(piece, w_key, preferred_element_type=jnp.float32)
    sums_value = jnp.dot(piece, w_value, preferred_element_type=jnp.float32)
    query = sums_query.astype(jnp.bfloat16)
    keys = sums_key.astype(jnp.bfloat16)
    values = sums_value.astype(jnp.bfloat16)
    query_blocks = query.reshape(blocks_here, block_rows, heads_here, head_size)
    stacked = jnp.stack([keys, values], 0)
    padded = extended(stacked, (("seq", 1),), WMAX * block_rows)
    span = 2 * WMAX + 1
    padded_blocks = padded.reshape(2, blocks_here + 2 * WMAX, block_rows, heads_here, head_size)
    window_kv = jnp.concatenate(
        [padded_blocks[:, offset : offset + blocks_here, None] for offset in range(span)], axis=2
    )
    window_kv = window_kv.reshape(2, blocks_here, span * block_rows, heads_here, head_size)
    distance = jnp.abs(jnp.arange(span, dtype=jnp.int32) - WMAX)
    window_valid = jnp.repeat(distance[None, :] <= windows[:, None], block_rows, axis=1)[
        None, :, None, :
    ]
    scores = (
        jnp.einsum(
            "bqhd,bkhd->bhqk", query_blocks, window_kv[0], preferred_element_type=jnp.float32
        )
        * score_scale
    )
    start_state = (
        jnp.full((blocks_here, heads_here, block_rows), NEGATIVE, jnp.float32),
        jnp.zeros((blocks_here, heads_here, block_rows), jnp.float32),
        jnp.zeros((blocks_here, heads_here, block_rows, head_size), jnp.float32),
    )
    top, total, accum, attention_weights = fold_scores(start_state, scores, window_valid)
    accum = jnp.einsum(
        "bhqk,bkhd->bhqd", attention_weights, window_kv[1], preferred_element_type=jnp.float32
    )
    state = (top, total, accum)
    all_valid = jnp.ones((1, 1, 1, 1), dtype=bool)
    targets = rand_blocks.reshape(-1)
    request_count = targets.shape[0]
    sources = targets // blocks_here
    order = jnp.arange(request_count, dtype=jnp.int32)
    earlier = (sources[:, None] == sources[None, :]) & (order[None, :] < order[:, None])
    ranks = jnp.sum(earlier.astype(jnp.int32), axis=1)
    slot_count = (request_count + seq_count - 1) // seq_count
    hits = (sources[:, None, None] == jnp.arange(seq_count, dtype=jnp.int32)[None, :, None]) & (
        ranks[:, None, None] == jnp.arange(slot_count, dtype=jnp.int32)[None, None, :]
    )
    slot_request = jnp.sum(jnp.where(hits, order[:, None, None], 0), axis=0)
    slot_live = jnp.any(hits, axis=0)
    row_steps = jnp.arange(block_rows, dtype=jnp.int32)
    owner_ids = jnp.arange(blocks_here, dtype=jnp.int32)
    piece = lax.all_gather(stacked, "seq", axis=1, tiled=True)
    count = piece.shape[1]
    picked = slot_request.reshape(-1)
    alive = slot_live.reshape(-1)
    slot_total = picked.shape[0]
    offset_rows = targets[picked][:, None] * block_rows + row_steps[None, :]
    chosen = piece[:, jnp.clip(offset_rows, 0, count - 1).reshape(-1)]
    chosen = chosen.reshape(2, slot_total * block_rows, heads_here, head_size)
    part_scores = (
        jnp.einsum("bqhd,khd->bhqk", query_blocks, chosen[0], preferred_element_type=jnp.float32)
        * score_scale
    )
    belongs = alive[None, :] & ((picked // picks_per_block)[None, :] == owner_ids[:, None])
    valid = jnp.repeat(belongs, block_rows, axis=1)[:, None, None, :]
    top_new, total_new, accum_new, part_weights = fold_scores(state, part_scores, valid)
    state = (
        top_new,
        total_new,
        accum_new
        + jnp.einsum("bhqk,khd->bhqd", part_weights, chosen[1], preferred_element_type=jnp.float32),
    )
    global_count = global_pos.shape[0]
    local_pos = global_pos - position * rows_here
    owned = (local_pos >= 0) & (local_pos < rows_here)
    row_ids = jnp.arange(rows_here, dtype=jnp.int32)
    selector = owned[:, None] & (local_pos[:, None] == row_ids[None, :])
    projected = jnp.concatenate([query, keys, values], axis=1)
    chosen_rows = jnp.dot(
        selector.astype(jnp.bfloat16), projected, preferred_element_type=jnp.float32
    )
    shared = lax.psum(chosen_rows.astype(jnp.bfloat16), "seq")
    g_query = shared[:, :group_width].reshape(global_count, heads_here, head_size)
    g_key = shared[:, group_width : 2 * group_width].reshape(global_count, heads_here, head_size)
    g_value = shared[:, 2 * group_width :].reshape(global_count, heads_here, head_size)
    global_score_rows = (
        jnp.einsum("bqhd,ghd->bhqg", query_blocks, g_key, preferred_element_type=jnp.float32)
        * score_scale
    )
    top, total, accum, attention_weights = fold_scores(state, global_score_rows, all_valid)
    accum = accum + jnp.einsum(
        "bhqg,ghd->bhqd", attention_weights, g_value, preferred_element_type=jnp.float32
    )
    sparse = (accum / total[..., None]).transpose(0, 2, 1, 3).reshape(rows_here, group_width)
    key_heads = keys.reshape(rows_here, heads_here, head_size)
    value_heads = values.reshape(rows_here, heads_here, head_size)
    g_scores = (
        jnp.einsum("ghd,thd->hgt", g_query, key_heads, preferred_element_type=jnp.float32)
        * score_scale
    )
    g_top = jnp.max(g_scores, axis=-1)
    g_probs = jnp.exp(g_scores - g_top[..., None])
    g_total = jnp.sum(g_probs, axis=-1)
    g_accum = jnp.einsum(
        "hgt,thd->hgd",
        g_probs.astype(jnp.bfloat16),
        value_heads,
        preferred_element_type=jnp.float32,
    )
    merged_top, merged_total, merged_accum = combined_all(
        (g_top, g_total, g_accum), "seq", join_states
    )
    finished = merged_accum / merged_total[..., None]
    placing = selector.astype(jnp.float32).T
    placed = jnp.einsum("tg,hgd->thd", placing, finished, precision=lax.Precision.HIGHEST)
    is_global = jnp.sum(placing, axis=1) > 0.5
    context = jnp.where(is_global[:, None], placed.reshape(rows_here, group_width), sparse).astype(
        jnp.bfloat16
    )
    term = jnp.dot(context, w_out, preferred_element_type=jnp.float32)
    return lax.psum_scatter(term.astype(jnp.bfloat16), "heads", scatter_dimension=1, tiled=True)


def solution(mesh):
    in_specs = (
        P("seq", "heads"),
        P(None, "heads"),
        P(None, "heads"),
        P(None, "heads"),
        P("heads", None),
        P("heads"),
        P("seq", None),
        P(),
    )
    out_specs = P("seq", "heads")
    return jax.shard_map(
        on_device, mesh=mesh, in_specs=in_specs, out_specs=out_specs, check_vma=False
    )
```

profile of v0, /device:TPU:96, one launch (start us, length us, event | category | flops | bytes accessed | tf_op | source)
XLA Modules:
  0.0 760.1 jit_solution(3525437572789591166)
XLA Ops:
  8.0 156.6 %all-gather.9.cloned.1.call-done = bf16[768,4096]{1,0:T(8,128)(2,1)} async-done(((bf16[768,256]{1,0:T(8,128)(2,1)}), bf16[768,4096]{1,0:T(8,128)(2,1)}) %all-gather.9.cloned.1.call-update) | async-done | bytes 6291472 | tf_op jit(solution)/shard_map/all_gather | solution.py:74
  164.6 5.4 convolution_convert_fusion.1
  175.7 144.2 %all-reduce.2.cloned.1.call-done = bf16[128,768]{1,0:T(8,128)(2,1)} async-done(((bf16[128,768]{1,0:T(8,128)(2,1)}), bf16[128,768]{1,0:T(8,128)(2,1)}) %all-reduce.2.cloned.1.call-update) | async-done | bytes 196624 | tf_op jit(solution)/shard_map/psum | solution.py:155
  336.6 5.4 collective-permute-start.1
  342.0 21.4 %all-gather.3 = f32[16,2,128]{2,1,0:T(2,128)S(1)} all-gather(f32[1,2,128]{2,1,0:T(2,128)S(1)} %bitcast.208), channel_id=2, replica_groups=mesh['seq'=16,'heads'=16] {'seq'}, dimensions={0}, use_global_device_ids=true | all-gather | bytes 17408 | tf_op jit(solution)/shard_map/all_gather | solution.py:29
  363.7 19.3 %all-gather.4 = f32[16,2,128]{2,1,0:T(2,128)S(1)} all-gather(f32[1,2,128]{2,1,0:T(2,128)S(1)} %bitcast.209), channel_id=3, replica_groups=mesh['seq'=16,'heads'=16] {'seq'}, dimensions={0}, use_global_device_ids=true | all-gather | bytes 17408 | tf_op jit(solution)/shard_map/all_gather | solution.py:29
  390.4 2.4 copy.143
  392.8 3.0 reshape.310
  399.4 4.7 fusion.94
  406.4 2.7 fusion.8
  409.1 3.1 slice.104
  412.2 16.8 %while.14 = (s32[]{:T(128)}, f32[2,128]{1,0:T(2,128)S(1)}, f32[2,128]{1,0:T(2,128)S(1)}, f32[2,128,128]{2,1,0:T(8,128)S(1)}, f32[15,2,128]{2,1,0:T(2,128)S(1)}, ...) while((s32[]{:T(128)}, f32[2,128]{1,0:T(2,128)S(1)}, f32[2,128]{1,0:T(2,128)S(1)}, ...), condition=%wide.region_5.6_spmd, body=%wide.region_4.5_spmd.sunk | while | flops 99842 | bytes 403557 | solution.py:32
  429.3 45.6 %all-gather.11.cloned.1.call-done = bf16[2,12288,256]{1,2,0:T(8,128)(2,1)} async-done(((bf16[2,768,256]{1,2,0:T(8,128)(2,1)}), bf16[2,12288,256]{1,2,0:T(8,128)(2,1)}) %all-gather.11.cloned.1.call-update) | async-done | bytes 12582928 | tf_op jit(solution)/shard_map/all_gather | solution.py:125
  474.9 30.9 %copy.151 = bf16[2,12288,256]{2,0,1:T(2,128)(2,1)} copy(bf16[2,12288,256]{1,2,0:T(8,128)(2,1)} %all-gather.11.cloned.1.call-done) | data formatting | bytes 25165824 | tf_op jit(solution)/shard_map/all_gather | solution.py:125
  505.8 37.2 %gather_fusion.1 = bf16[4096,2,256]{2,1,0:T(2,128)(2,1)} fusion(bf16[2,12288,256]{2,0,1:T(2,128)(2,1)} %copy.151, s32[4096]{0:T(1024)S(1)} %copy-done.8), kind=kCustom, calls=%fused_computation.1 | custom fusion | bytes 8404992 | tf_op jit(solution)/shard_map/gather | solution.py:131
  543.0 9.9 %fusion.93 = (bf16[1,4096,256]{2,0,1:T(2,128)(2,1)}, bf16[1,4096,256]{2,0,1:T(2,128)(2,1)}) fusion(bf16[2,4096,256]{2,0,1:T(2,128)(2,1)} %bitcast.183), kind=kLoop, calls=%fused_computation.149 | loop fusion | bytes 8388608 | tf_op jit(solution)/shard_map/slice | solution.py:134
  552.9 9.8 %copy.152 = bf16[1,4096,256]{1,2,0:T(8,128)(2,1)} copy(bf16[1,4096,256]{2,0,1:T(2,128)(2,1)} %get-tuple-element.72) | data formatting | bytes 4194304 | tf_op jit(solution)/shard_map/slice | solution.py:134
  562.7 9.8 %copy.160 = bf16[1,4096,256]{1,2,0:T(8,128)(2,1)} copy(bf16[1,4096,256]{2,0,1:T(2,128)(2,1)} %get-tuple-element.73) | data formatting | bytes 4194304 | tf_op jit(solution)/shard_map/slice | solution.py:144
  572.4 7.7 %fusion.3 = (f32[6,2,128]{2,0,1:T(8,128)S(1)}, f32[2,4096,6,128]{3,1,2,0:T(8,128)S(1)}) fusion(pred[6,4096]{1,0:T(8,128)(4,1)S(1)} %bitcast.199, bf16[4096,2,128,1]{0,2,3,1:T(8,128)(2,1)} %bitcast.195, bf16[6,128,2,128]{3,2,1,0:T(2,128)(2,1)S(1)} %copy-done.3), kind=kOutput, calls=%fused_computation.13 | convolution fusion | flops 1629485568 | bytes 27686912 | tf_op jit(solution)/shard_map/bqhd,khd->bhqk/dot_general | solution.py:134
  581.6 13.8 %fusion.4 = (f32[6,2,128]{2,0,1:T(8,128)S(1)}, bf16[6,2,128,4096]{2,3,0,1:T(8,128)(2,1)}) fusion(f32[2,4096,6,128]{3,1,2,0:T(8,128)S(1)} %get-tuple-element.89, f32[6,2,128]{2,0,1:T(8,128)S(1)} %copy.162, pred[6,4096]{1,0:T(8,128)(4,1)S(1)} %bitcast.200), kind=kLoop, calls=%fused_computation.14 | loop fusion | flops 37747200 | bytes 37785600 | tf_op jit(solution)/shard_map/reduce_sum | solution.py:44
  595.4 10.6 %fusion.18 = f32[6,128,2,128]{3,1,2,0:T(8,128)} fusion(bf16[4096,2,128,1]{0,2,1,3:T(8,128)(2,1)S(1)} %bitcast.194, bf16[6,2,128,4096]{2,3,0,1:T(8,128)(2,1)} %get-tuple-element.71), kind=kOutput, calls=%fused_computation.31 | convolution fusion | flops 1610612736 | bytes 15466496 | tf_op jit(solution)/shard_map/bhqk,khd->bhqd/dot_general | solution.py:144
  606.0 3.2 fusion.33
  610.7 4.5 convolution_convert_fusion
  615.2 138.4 %reduce-scatter.2.cloned.1.call-done = bf16[768,256]{1,0:T(8,128)(2,1)} async-done(((bf16[768,4096]{1,0:T(8,128)(2,1)}), bf16[768,256]{1,0:T(8,128)(2,1)}) %reduce-scatter.2.cloned.1.call-update) | async-done | bytes 393232 | tf_op jit(solution)/shard_map/reduce_scatter | solution.py:194
  (169 shorter events, 56.9 us)
Async XLA Ops:
  6.5 604.1 %copy-start = (bf16[256,4096]{1,0:T(8,128)(2,1)S(1)}, bf16[256,4096]{1,0:T(8,128)(2,1)}, u32[]{:S(2)}) copy-start(bf16[256,4096]{1,0:T(8,128)(2,1)} %param.14) | copy-start | bytes 6291460
  6.5 158.0 %all-gather.9.cloned.1.call-start = ((), (), s32[]{:S(2)}) async-start(), calls=%async_computation.1 | async-start | bytes 6684672 | tf_op jit(solution)/shard_map/all_gather | solution.py:74
  7.3 312.6 %all-reduce.2.cloned.1.call-start = ((), (), s32[]{:S(2)}) async-start(), calls=%async_computation.2 | async-start | bytes 393216 | tf_op jit(solution)/shard_map/psum | solution.py:155
  8.0 321.7 %copy-start.15 = (pred[128]{0:T(512)(128)(4,1)}, pred[128]{0:T(512)(128)(4,1)S(1)}, u32[]{:S(2)}) copy-start(pred[128]{0:T(512)(128)(4,1)S(1)} %get-tuple-element.68) | copy-start | bytes 388
  8.0 321.7 %copy-start.17 = (s32[128]{0:T(128)}, s32[128]{0:T(128)S(1)}, u32[]{:S(2)}) copy-start(s32[128]{0:T(128)S(1)} %get-tuple-element.69) | copy-start | bytes 1540
  164.6 5.4 copy-start.20
  164.6 5.8 copy-start.21
  174.4 147.1 %copy-start.6 = (bf16[768,256]{0,1:T(8,128)(2,1)}, bf16[768,256]{0,1:T(8,128)(2,1)S(1)}, u32[]{:S(2)}) copy-start(bf16[768,256]{0,1:T(8,128)(2,1)S(1)} %convolution_convert_fusion.3) | copy-start | bytes 1179652
  174.4 151.6 %copy-start.23 = (s32[2]{0:T(128)S(1)}, s32[2]{0:T(128)}, u32[]{:S(2)}) copy-start(s32[2]{0:T(128)} %param.15) | copy-start | bytes 28
  174.4 152.3 %copy-start.14 = (s32[6,3]{0,1:T(4,128)S(1)}, s32[6,3]{0,1:T(4,128)}, u32[]{:S(2)}) copy-start(s32[6,3]{0,1:T(4,128)} %param.16) | copy-start | bytes 220
  175.7 233.4 %all-gather.13.cloned.1.call-start = ((), (), s32[]{:S(2)}) async-start(), calls=%async_computation.5 | async-start | bytes 2228224 | tf_op jit(solution)/shard_map/all_gather | solution.py:29
  323.9 151.0 %all-gather.11.cloned.1.call-start = ((), (), s32[]{:S(2)}) async-start(), calls=%async_computation.3 | async-start | bytes 13369344 | tf_op jit(solution)/shard_map/all_gather | solution.py:125
  325.9 427.6 %reduce-scatter.2.cloned.1.call-start = ((), (), s32[]{:S(2)}) async-start(), calls=%async_computation.4 | async-start | bytes 6684672 | tf_op jit(solution)/shard_map/reduce_scatter | solution.py:194
  336.6 51.5 %collective-permute-start = (bf16[2,256,256]{1,2,0:T(8,128)(2,1)}, bf16[2,256,256]{1,2,0:T(8,128)(2,1)S(1)}, u32[]{:S(2)}, u32[]{:S(2)}) collective-permute-start(bf16[2,256,256]{1,2,0:T(8,128)(2,1)} %get-tuple-element.78), channel_id=1, source_target_pairs={{0,16},{16,32},{32,48},{48,64},{64,80},{80,96},{96,112},{112,128},... | collective-permute-start | bytes 786440 | tf_op jit(solution)/shard_map/ppermute | solution.py:20
  336.6 51.5 %collective-permute-start.1 = (bf16[2,256,256]{1,2,0:T(8,128)(2,1)}, bf16[2,256,256]{1,2,0:T(8,128)(2,1)}, u32[]{:S(2)}, u32[]{:S(2)}) collective-permute-start(bf16[2,256,256]{1,2,0:T(8,128)(2,1)} %get-tuple-element.79), channel_id=1, source_target_pairs={{16,0},{32,16},{48,32},{64,48},{80,64},{96,80},{112,96},{128,112},... | collective-permute-start | bytes 786440 | tf_op jit(solution)/shard_map/ppermute | solution.py:23
  363.4 20.1 %copy-start.10 = (f32[16,2,128]{2,1,0:T(2,128)}, f32[16,2,128]{2,1,0:T(2,128)S(1)}, u32[]{:S(2)}) copy-start(f32[16,2,128]{2,1,0:T(2,128)S(1)} %all-gather.3) | copy-start | bytes 49156
  406.4 5.8 slice-start.1
  406.4 5.8 slice-start.2
  406.4 5.8 copy-start.12
  429.3 76.6 %copy-start.8 = (s32[4096]{0:T(1024)S(1)}, s32[4096]{0:T(1024)}, u32[]{:S(2)}) copy-start(s32[4096]{0:T(1024)} %broadcast_clamp_fusion) | copy-start | bytes 49156
  562.7 9.8 %copy-start.7 = (pred[1,6,32,128]{3,1,2,0:T(8,128)(4,1)S(1)}, pred[1,6,32,128]{3,1,2,0:T(8,128)(4,1)}, u32[]{:S(2)}) copy-start(pred[1,6,32,128]{3,1,2,0:T(8,128)(4,1)} %copy.235) | copy-start | bytes 73732
  572.4 7.8 %copy-start.4 = (f32[6,2,128,128]{2,3,0,1:T(8,128)S(1)}, f32[6,2,128,128]{2,3,0,1:T(8,128)}, u32[]{:S(2)}) copy-start(f32[6,2,128,128]{2,3,0,1:T(8,128)} %get-tuple-element.87) | copy-start | bytes 2359300
  572.4 7.9 %copy-start.1 = (f32[6,2,128,640]{3,2,1,0:T(8,128)S(1)}, f32[6,2,128,640]{3,2,1,0:T(8,128)}, u32[]{:S(2)}) copy-start(f32[6,2,128,640]{3,2,1,0:T(8,128)} %get-tuple-element.91) | copy-start | bytes 11796484
  581.5 13.8 %copy-start.5 = (bf16[1,4096,256]{1,2,0:T(8,128)(2,1)S(1)}, bf16[1,4096,256]{1,2,0:T(8,128)(2,1)}, u32[]{:S(2)}) copy-start(bf16[1,4096,256]{1,2,0:T(8,128)(2,1)} %copy.160) | copy-start | bytes 6291460
  (10 other events, 18.2 us)
Sparse Core Ops, SparseCore 0:
  9.1 155.4 all-gather.8
  175.8 144.0 all-reduce.1
  324.0 53.9 all-gather.12
  381.0 93.8 all-gather.10
  615.3 138.1 reduce-scatter.1
where the time goes:
time: 764 us; the launch traced here: 760 us
  waiting for transfers between devices  485 us (63%)
  local copies, waits for them, and re-layouts  129 us (17%)
  matrix products  44.7 us (6%)
  other arithmetic  40.7 us (5%)
  blocking collectives  40.7 us (5%)
  between operations  13.7 us (2%)
    all_gather x1, waiting for transfers between devices, on_device(): piece = lax.all_gather(activations, 'heads', axis=1, tiled=True)  157 us
    psum x1, waiting for transfers between devices, on_device(): shared = lax.psum(chosen_rows.astype(jnp.bfloat16), 'seq')  144 us
    reduce_scatter x1, waiting for transfers between devices, on_device(): lax.psum_scatter(term.astype(jnp.bfloat16), 'heads', scatter_dimension=1,...  138 us
    all_gather x1, waiting for transfers between devices, on_device(): piece = lax.all_gather(stacked, 'seq', axis=1, tiled=True)  45.6 us
    all_gather x2, blocking collectives, combined_all(): pieces = jax.tree.map(lambda part: lax.all_gather(part, axis), value)  40.7 us
    gather x1, local copies, waits for them, and re-layouts, on_device(): chosen = piece[:, jnp.clip(offset_rows, 0, count - 1).reshape(-1)]  37.2 us
    all_gather x1, local copies, waits for them, and re-layouts, on_device(): piece = lax.all_gather(stacked, 'seq', axis=1, tiled=True)  30.9 us
    slice x2, local copies, waits for them, and re-layouts, on_device(): chosen[0]  19.7 us
  transfers between devices with their start and end apart: 7, of which 4 were waited for; matrix products, arithmetic and copies ran while one was open for 8% of the time, Pallas kernels for 0%

commit v1 on v0

v1 whole, which is shorter than its diff:
```python
import math

import jax
import jax.numpy as jnp
from jax import lax
from jax.experimental import pallas as pl
from jax.experimental.pallas import tpu as pltpu
from jax.sharding import PartitionSpec as P

WMAX = 2
SPAN = 2 * WMAX + 1
R = 3
PICKS = SPAN + R
BLK = 128
BLK_DEV = 6
ROWS = BLK * BLK_DEV
GMAX = 32
G = 128
HD = 128
HEADS_DEV = 2
WIDTH = HD * HEADS_DEV
N_SEQ = 16
N_HEADS = 16
NBLK = N_SEQ * BLK_DEV
UNIT = ROWS + GMAX
NEGATIVE = -1e30
SCALE = 1.0 / math.sqrt(HD)
F32 = jnp.float32
BF16 = jnp.bfloat16

HEAD_SLOTS = (
    ((0, 0), (0, 0), (0, 0)),
    ((-1, 0), (1, 0), (-1, 0)),
    ((-2, 0), (2, 0), (1, 0)),
    ((-3, 0), (1, 1), (-2, 0)),
    ((-2, 1), (2, 1), (-4, 0)),
)
Z_UP = [(h, (h + 2) % 16) for h in range(16)]
Z_DOWN = [(h, (h - 2) % 16) for h in range(16)]
PAIR = [(h, h ^ 1) for h in range(16)]


def head_order():
    items = [(0, 0)]
    for up, down, across in HEAD_SLOTS:
        items += [
            (up[0] - 1, up[1]),
            (down[0] + 1, down[1]),
            (across[0], across[1] ^ 1),
        ]
    return items


Y_UP = [(s, (s // 8) * 8 + (s % 8 + 2) % 8) for s in range(16)]
Y_DOWN = [(s, (s // 8) * 8 + (s % 8 - 2) % 8) for s in range(16)]
HALF = [(s, s ^ 8) for s in range(16)]
CORE = [(s, s ^ 1) for s in range(16)]


def vmem():
    return pl.BlockSpec(memory_space=pltpu.VMEM)


def project_kernel(count, first, last, ids, *refs):
    xs, refs = refs[:count], refs[count:]
    ws, refs = refs[: 3 * count], refs[3 * count :]
    if not first:
        acc, refs = refs[0], refs[1:]
    if last:
        sel_ref, q_out, kv_out = refs
    else:
        (out,) = refs
    parts = []
    for j in range(3):
        total = None if first else acc[:, j * WIDTH : (j + 1) * WIDTH]
        for i in range(count):
            term = jnp.dot(
                xs[i][...], ws[3 * i + j][...], preferred_element_type=F32
            )
            total = term if total is None else total + term
        if last:
            parts.append(total.astype(BF16))
        else:
            out[:, j * WIDTH : (j + 1) * WIDTH] = total
    if last:
        columns = lax.broadcasted_iota(jnp.int32, (GMAX, ROWS), 1)
        pick = jnp.where(columns == sel_ref[...], 1.0, 0.0).astype(BF16)
        for j, part in enumerate(parts):
            chosen = jnp.dot(pick, part, preferred_element_type=F32).astype(BF16)
            dest = q_out if j == 0 else kv_out
            low = max(j - 1, 0) * WIDTH
            dest[:ROWS, low : low + WIDTH] = part
            dest[ROWS:, low : low + WIDTH] = chosen


def project(ids, offset, xs, weights, acc, selected=None):
    count = len(xs)
    first, last = acc is None, selected is not None
    full = lambda shape: pl.BlockSpec(shape, lambda g, ids: (0, 0))
    in_specs = [full((ROWS, WIDTH)) for _ in xs]
    operands = list(xs)
    for i in range(count):
        for w in weights:
            in_specs.append(
                pl.BlockSpec((WIDTH, WIDTH), lambda g, ids, i=i: (ids[offset + i], 0))
            )
            operands.append(w)
    aliases = {}
    if not first:
        in_specs.append(full((ROWS, 3 * WIDTH)))
        operands.append(acc)
        if not last:
            aliases = {len(operands): 0}
    if last:
        in_specs.append(full((GMAX, 1)))
        operands.append(selected)
        out_shape = (
            jax.ShapeDtypeStruct((UNIT, WIDTH), BF16),
            jax.ShapeDtypeStruct((UNIT, 2 * WIDTH), BF16),
        )
        out_specs = (full((UNIT, WIDTH)), full((UNIT, 2 * WIDTH)))
    else:
        out_shape = jax.ShapeDtypeStruct((ROWS, 3 * WIDTH), F32)
        out_specs = full((ROWS, 3 * WIDTH))

    def body(*refs):
        project_kernel(count, first, last, *refs)

    return pl.pallas_call(
        body,
        out_shape=out_shape,
        grid_spec=pltpu.PrefetchScalarGridSpec(
            num_scalar_prefetch=1, grid=(1,), in_specs=in_specs, out_specs=out_specs
        ),
        input_output_aliases=aliases,
        compiler_params=pltpu.CompilerParams(vmem_limit_bytes=40 << 20),
        cost_estimate=pl.CostEstimate(
            flops=2 * count * ROWS * WIDTH * 3 * WIDTH,
            transcendentals=0,
            bytes_accessed=6 << 20,
        ),
        name="project",
    )(ids, *operands)


def combine_kernel(count, first, last, ids, *refs):
    cs, refs = refs[:count], refs[count:]
    ws, refs = refs[:count], refs[count:]
    total = None
    if not first:
        acc, refs = refs[0], refs[1:]
        total = acc[...]
    (out,) = refs
    for i in range(count):
        part = jnp.dot(cs[i][...], ws[i][0], preferred_element_type=F32)
        part = part.astype(BF16).astype(F32)
        total = part if total is None else total + part
    out[...] = total.astype(out.dtype)


def combine(ids, offset, cs, w_parts, acc, last=False):
    count = len(cs)
    first = acc is None
    full = lambda shape: pl.BlockSpec(shape, lambda g, ids: (0, 0))
    in_specs = [full((ROWS, WIDTH)) for _ in cs]
    operands = list(cs)
    for i in range(count):
        in_specs.append(
            pl.BlockSpec(
                (1, WIDTH, WIDTH), lambda g, ids, i=i: (ids[offset + i], 0, 0)
            )
        )
        operands.append(w_parts)
    aliases = {}
    if not first:
        in_specs.append(full((ROWS, WIDTH)))
        operands.append(acc)
        if not last:
            aliases = {len(operands): 0}

    def body(*refs):
        combine_kernel(count, first, last, *refs)

    return pl.pallas_call(
        body,
        out_shape=jax.ShapeDtypeStruct((ROWS, WIDTH), BF16 if last else F32),
        grid_spec=pltpu.PrefetchScalarGridSpec(
            num_scalar_prefetch=1,
            grid=(1,),
            in_specs=in_specs,
            out_specs=full((ROWS, WIDTH)),
        ),
        input_output_aliases=aliases,
        compiler_params=pltpu.CompilerParams(vmem_limit_bytes=40 << 20),
        cost_estimate=pl.CostEstimate(
            flops=2 * count * ROWS * WIDTH * WIDTH,
            transcendentals=0,
            bytes_accessed=3 << 20,
        ),
        name="combine",
    )(ids, *operands)


def gather_heads(own):
    have = {(0, 0): own}
    for up, down, across in HEAD_SLOTS:
        got = [
            lax.ppermute(have[up], "heads", Z_UP),
            lax.ppermute(have[down], "heads", Z_DOWN),
            lax.ppermute(have[across], "heads", PAIR),
        ]
        have[(up[0] - 1, up[1])] = got[0]
        have[(down[0] + 1, down[1])] = got[1]
        have[(across[0], across[1] ^ 1)] = got[2]
        yield got


def gather_seq(own):
    up = lambda a: lax.ppermute(a, "seq", Y_UP)
    down = lambda a: lax.ppermute(a, "seq", Y_DOWN)
    half = lambda a: lax.ppermute(a, "seq", HALF)
    have = {(0, 0): own}
    have[0, 3] = up(own)
    have[0, 1] = down(own)
    have[1, 0] = half(own)
    have[0, 2] = up(have[0, 3])
    have[1, 1] = down(have[1, 0])
    have[1, 3] = half(have[0, 3])
    pieces = [(dx * 8 + dy * 2, 0, piece) for (dx, dy), piece in have.items()]
    cuts = (0, 272, 544, UNIT)
    last = (
        up(lax.slice_in_dim(have[1, 3], cuts[0], cuts[1], axis=0)),
        down(lax.slice_in_dim(have[1, 1], cuts[1], cuts[2], axis=0)),
        half(lax.slice_in_dim(have[0, 2], cuts[2], cuts[3], axis=0)),
    )
    for i, piece in enumerate(last):
        pieces.append((12, cuts[i], piece))
    pieces += [
        (slot + 1, row, lax.ppermute(piece, "seq", CORE)) for slot, row, piece in pieces
    ]
    return pieces


def attention_kernel(layout, slots, rows, windows, q_ref, gslot_ref, sel_ref, *refs):
    count = len(layout)
    pieces, (out_ref, buf, sems) = refs[:count], refs[count:]
    copies = []
    for i, (slot, row) in enumerate(layout):
        size = pieces[i].shape[0]
        copies.append(
            pltpu.make_async_copy(
                pieces[i], buf.at[slot, pl.ds(row, size)], sems.at[i]
            )
        )
    for copy in copies:
        copy.start()
    for copy in copies:
        copy.wait()

    dims = (((1,), (1,)), ((), ()))
    found = jnp.concatenate([buf[i, ROWS:UNIT, :] for i in range(N_SEQ)], axis=0)
    where = lax.broadcasted_iota(jnp.int32, (G, N_SEQ * GMAX), 1)
    pick = jnp.where(where == gslot_ref[...], 1.0, 0.0).astype(BF16)
    g_kv = jnp.dot(pick, found, preferred_element_type=F32).astype(BF16)

    steps = lax.broadcasted_iota(jnp.int32, (ROWS, GMAX), 0)
    place = jnp.where(steps == sel_ref[...], 1.0, 0.0)
    is_global = jnp.sum(place, axis=1, keepdims=True) > 0.5
    place = place.astype(BF16)

    for head in range(HEADS_DEV):
        low, high = head * HD, (head + 1) * HD
        vlow, vhigh = WIDTH + low, WIDTH + high
        g_query = q_ref[ROWS:UNIT, low:high]
        g_scores = [
            lax.dot_general(
                g_query, buf[i, :ROWS, low:high], dims, preferred_element_type=F32
            )
            * SCALE
            for i in range(N_SEQ)
        ]
        top = g_scores[0]
        for s in g_scores[1:]:
            top = jnp.maximum(top, s)
        top = jnp.max(top, axis=1, keepdims=True)
        sums = jnp.zeros((GMAX, ROWS), F32)
        acc = jnp.zeros((GMAX, HD), F32)
        for i in range(N_SEQ):
            p = jnp.exp(g_scores[i] - top)
            sums = sums + p
            acc = acc + jnp.dot(
                p.astype(BF16), buf[i, :ROWS, vlow:vhigh], preferred_element_type=F32
            )
        total = jnp.sum(sums, axis=1, keepdims=True)
        g_context = (acc / total).astype(BF16)
        placed = jnp.dot(place, g_context, preferred_element_type=F32)
        wide = windows[head] >= WMAX
        for b in range(BLK_DEV):
            query = q_ref[b * BLK : (b + 1) * BLK, low:high]
            where_kv = [
                (slots[b * PICKS + j], pl.multiple_of(rows[b * PICKS + j], BLK))
                for j in range(PICKS)
            ]
            scores = []
            for j, (slot, row) in enumerate(where_kv):
                s = (
                    lax.dot_general(
                        query,
                        buf[slot, pl.ds(row, BLK), low:high],
                        dims,
                        preferred_element_type=F32,
                    )
                    * SCALE
                )
                if j == 0 or j == SPAN - 1:
                    s = jnp.where(wide, s, NEGATIVE)
                scores.append(s)
            scores.append(
                lax.dot_general(
                    query, g_kv[:, low:high], dims, preferred_element_type=F32
                )
                * SCALE
            )
            top = scores[0]
            for s in scores[1:]:
                top = jnp.maximum(top, s)
            top = jnp.max(top, axis=1, keepdims=True)
            sums = None
            acc = None
            for j, s in enumerate(scores):
                p = jnp.exp(s - top)
                sums = p if sums is None else sums + p
                if j < PICKS:
                    slot, row = where_kv[j]
                    v = buf[slot, pl.ds(row, BLK), vlow:vhigh]
                else:
                    v = g_kv[:, vlow:vhigh]
                term = jnp.dot(p.astype(BF16), v, preferred_element_type=F32)
                acc = term if acc is None else acc + term
            context = acc / jnp.sum(sums, axis=1, keepdims=True)
            span = slice(b * BLK, (b + 1) * BLK)
            out_ref[span, low:high] = jnp.where(
                is_global[span], placed[span], context
            ).astype(BF16)


def attention(slots, rows, windows, query, gslot, selected, pieces):
    layout = [(slot, row) for slot, row, _ in pieces]
    smem_blocks = [vmem()] * 3 + [pl.BlockSpec(memory_space=pl.ANY)] * len(pieces)

    def body(*refs):
        attention_kernel(layout, *refs)

    return pl.pallas_call(
        body,
        out_shape=jax.ShapeDtypeStruct((ROWS, WIDTH), BF16),
        grid_spec=pltpu.PrefetchScalarGridSpec(
            num_scalar_prefetch=3,
            grid=(),
            in_specs=smem_blocks,
            out_specs=vmem(),
            scratch_shapes=[
                pltpu.VMEM((N_SEQ, UNIT, 2 * WIDTH), BF16),
                pltpu.SemaphoreType.DMA((len(pieces),)),
            ],
        ),
        compiler_params=pltpu.CompilerParams(vmem_limit_bytes=48 << 20),
        cost_estimate=pl.CostEstimate(
            flops=2 << 30, transcendentals=3 << 20, bytes_accessed=14 << 20
        ),
        name="attention",
    )(slots, rows, windows, query, gslot, selected, *[p for _, _, p in pieces])


def on_device(
    activations, w_query, w_key, w_value, w_out, windows, rand_blocks, global_pos
):
    me = lax.axis_index("heads")
    here = lax.axis_index("seq")
    items = head_order()
    shifts = jnp.array([d for d, _ in items], jnp.int32)
    flips = jnp.array([e for _, e in items], jnp.int32)
    ids = (me // 2 + shifts + 8) % 8 * 2 + (me % 2 + flips) % 2

    def slot_of(seq):
        dx = (seq // 8 + here // 8) % 2
        dy = (seq // 2 % 4 - here // 2 % 4 + 4) % 4
        return dx * 8 + dy * 2 + (seq + here) % 2

    blocks = jnp.arange(BLK_DEV, dtype=jnp.int32)[:, None] + here * BLK_DEV
    offsets = jnp.arange(SPAN, dtype=jnp.int32)[None, :] - WMAX
    near = (blocks + offsets + NBLK) % NBLK
    named = jnp.concatenate([near, rand_blocks], axis=1).reshape(-1)
    key_slots = slot_of(named // BLK_DEV)
    key_rows = named % BLK_DEV * BLK

    owners = global_pos // ROWS
    order = jnp.arange(G, dtype=jnp.int32)
    earlier = (owners[:, None] == owners[None, :]) & (order[None, :] < order[:, None])
    ranks = jnp.sum(earlier.astype(jnp.int32), axis=1)
    gslot = (slot_of(owners) * GMAX + ranks)[:, None]
    mine = (owners == here)[None, :] & (
        ranks[None, :] == jnp.arange(GMAX, dtype=jnp.int32)[:, None]
    )
    selected = jnp.max(jnp.where(mine, (global_pos - here * ROWS)[None, :], -1), axis=1)

    weights = (w_query, w_key, w_value)
    acc = project(ids, 0, [activations], weights, None)
    slots = list(gather_heads(activations))
    for t, got in enumerate(slots[:-1]):
        acc = project(ids, 1 + 3 * t, got, weights, acc)
    query, unit = project(
        ids, 13, slots[-1], weights, acc, selected=selected[:, None]
    )

    w_blocks = w_out.reshape(WIDTH, N_HEADS, WIDTH).transpose(1, 0, 2)
    w_blocks, unit = lax.optimization_barrier((w_blocks, unit))
    pieces = gather_seq(unit)
    w_parts = lax.all_to_all(w_blocks, "heads", 0, 0)

    ctx = attention(
        key_slots, key_rows, windows, query, gslot, selected[None, :], pieces
    )
    out = combine(ids, 0, [ctx], w_parts, None)
    slots = list(gather_heads(ctx))
    for t, got in enumerate(slots):
        out = combine(ids, 1 + 3 * t, got, w_parts, out, last=t == len(slots) - 1)
    return out


def solution(mesh):
    in_specs = (
        P("seq", "heads"),
        P(None, "heads"),
        P(None, "heads"),
        P(None, "heads"),
        P("heads", None),
        P("heads"),
        P("seq", None),
        P(),
    )
    out_specs = P("seq", "heads")
    return jax.shard_map(
        on_device, mesh=mesh, in_specs=in_specs, out_specs=out_specs, check_vma=False
    )
```

time: 764 us -> 270 us (0.35)
  waiting for transfers between devices: 485 us -> 116 us
  local copies, waits for them, and re-layouts: 129 us -> 23.8 us
  starting transfers between devices: 5.53 us -> 83.3 us
  matrix products: 44.7 us -> 0 us
  Pallas kernels: 0 us -> 41.9 us
  blocking collectives: 40.7 us -> 0 us
  other arithmetic: 40.7 us -> 2.61 us
  between operations: 13.7 us -> 0.58 us
    all_gather x3 -> x0, waiting for transfers between devices: 202 us -> none  [the longest x1 157 us: on_device(): piece = lax.all_gather(activations, 'heads', axis=1, tiled=True)]
    psum x1 -> x0, waiting for transfers between devices: 144 us -> none  [on_device(): shared = lax.psum(chosen_rows.astype(jnp.bfloat16), 'seq')]
    reduce_scatter x1 -> x0, waiting for transfers between devices: 138 us -> none  [on_device(): lax.psum_scatter(term.astype(jnp.bfloat16), 'heads', scatter_dimension=1,...]
    ppermute x2 -> x49, waiting for transfers between devices: 0.01 us -> 116 us  [the longest x10 38 us: gather_heads(): lax.ppermute(have[up], 'heads', Z_UP)]
    ppermute x2 -> x49, starting transfers between devices: 5.36 us -> 78.1 us  [the longest x10 35.5 us: gather_heads(): lax.ppermute(have[up], 'heads', Z_UP)]
    dot_general x13 -> x0, matrix products: 44.1 us -> none  [the longest x1 10.6 us: on_device(): jnp.einsum('bhqk,khd->bhqd', part_weights, chosen[1], preferred_element_t...]
    pallas_call x0 -> x13, Pallas kernels: none -> 41.9 us  [the longest x1 15.6 us: attention(): pl.pallas_call(body, out_shape=jax.ShapeDtypeStruct((ROWS, WIDTH), BF16),...]
    all_gather x2 -> x0, blocking collectives: 40.7 us -> none  [combined_all(): pieces = jax.tree.map(lambda part: lax.all_gather(part, axis), value)]
  transfers between devices with their start and end apart: 7 -> 50, of which waited for: 4 -> 21; matrix products, arithmetic and copies ran while one was open for 8% -> 6% of each run, Pallas kernels for 0% -> 13%
where the time goes in v1:
time: 270 us; the launch traced here: 268 us
  waiting for transfers between devices  116 us (43%)
  starting transfers between devices  83.3 us (31%)
  Pallas kernels  41.9 us (16%)
  local copies, waits for them, and re-layouts  23.8 us (9%)
    ppermute x10, waiting for transfers between devices, gather_heads(): lax.ppermute(have[up], 'heads', Z_UP)  38 us
    ppermute x3, waiting for transfers between devices, gather_seq(): half = lambda a: lax.ppermute(a, 'seq', HALF)  36.2 us
    ppermute x10, starting transfers between devices, gather_heads(): lax.ppermute(have[up], 'heads', Z_UP)  35.5 us
    ppermute x10, starting transfers between devices, gather_heads(): lax.ppermute(have[across], 'heads', PAIR)  22.7 us
    ppermute x10, waiting for transfers between devices, gather_heads(): lax.ppermute(have[down], 'heads', Z_DOWN)  19.1 us
    pallas_call x1, Pallas kernels, attention(): pl.pallas_call(body, out_shape=jax.ShapeDtypeStruct((ROWS, WIDTH), BF16),...  15.6 us
    ppermute x3, waiting for transfers between devices, gather_seq(): up = lambda a: lax.ppermute(a, 'seq', Y_UP)  14.8 us
    pallas_call x6, Pallas kernels, project(): pl.pallas_call(body, out_shape=out_shape, grid_spec=pltpu.PrefetchScalarG...  14.8 us
  transfers between devices with their start and end apart: 50, of which 21 were waited for; matrix products, arithmetic and copies ran while one was open for 6% of the time, Pallas kernels for 13%

profile of v1, /device:TPU:96, one launch (start us, length us, event | category | flops | bytes accessed | tf_op | source)
XLA Modules:
  0.0 268.5 jit_solution(7297804161086054233)
XLA Ops:
  3.1 8.7 %collective-permute-done.refs_1_ = bf16[768,256]{1,0:T(8,128)(2,1)S(1)} collective-permute-done((bf16[768,256]{1,0:T(8,128)(2,1)}, bf16[768,256]{1,0:T(8,128)(2,1)S(1)}, u32[]{:S(2)}, u32[]{:S(2)}) %collective-permute-start) | collective-permute-done | bytes 393248 | tf_op jit(solution)/shard_map/ppermute | solution.py:208
  11.8 3.6 %collective-permute-start.1 = (bf16[768,256]{1,0:T(8,128)(2,1)S(1)}, bf16[768,256]{1,0:T(8,128)(2,1)S(1)}, u32[]{:S(2)}, u32[]{:S(2)}) collective-permute-start(bf16[768,256]{1,0:T(8,128)(2,1)S(1)} %collective-permute-done.refs_1_), channel_id=1, source_target_pairs={{0,2},{1,3},{2,4},{3,5},{4,6},{5,7},{6,8},{7,9},{8,10},{9,11},{10,... | collective-permute-start | bytes 1179656 | tf_op jit(solution)/shard_map/ppermute | solution.py:208
  16.9 6.0 %collective-permute-done.1.refs_1_ = bf16[768,256]{1,0:T(8,128)(2,1)S(1)} collective-permute-done((bf16[768,256]{1,0:T(8,128)(2,1)S(1)}, bf16[768,256]{1,0:T(8,128)(2,1)S(1)}, u32[]{:S(2)}, u32[]{:S(2)}) %collective-permute-start.1) | collective-permute-done | bytes 393248 | tf_op jit(solution)/shard_map/ppermute | solution.py:208
  22.9 3.7 %collective-permute-start.8 = (bf16[768,256]{1,0:T(8,128)(2,1)S(1)}, bf16[768,256]{1,0:T(8,128)(2,1)S(1)}, u32[]{:S(2)}, u32[]{:S(2)}) collective-permute-start(bf16[768,256]{1,0:T(8,128)(2,1)S(1)} %collective-permute-done.1.refs_1_), channel_id=1, source_target_pairs={{0,2},{1,3},{2,4},{3,5},{4,6},{5,7},{6,8},{7,9},{8,10},{9,11},{10,... | collective-permute-start | bytes 1179656 | tf_op jit(solution)/shard_map/ppermute | solution.py:208
  29.5 3.7 %collective-permute-done.8.refs_1_ = bf16[768,256]{1,0:T(8,128)(2,1)S(1)} collective-permute-done((bf16[768,256]{1,0:T(8,128)(2,1)S(1)}, bf16[768,256]{1,0:T(8,128)(2,1)S(1)}, u32[]{:S(2)}, u32[]{:S(2)}) %collective-permute-start.8) | collective-permute-done | bytes 393248 | tf_op jit(solution)/shard_map/ppermute | solution.py:208
  33.2 3.7 %collective-permute-start.9 = (bf16[768,256]{1,0:T(8,128)(2,1)S(1)}, bf16[768,256]{1,0:T(8,128)(2,1)}, u32[]{:S(2)}, u32[]{:S(2)}) collective-permute-start(bf16[768,256]{1,0:T(8,128)(2,1)S(1)} %collective-permute-done.8.refs_1_), channel_id=1, source_target_pairs={{0,2},{1,3},{2,4},{3,5},{4,6},{5,7},{6,8},{7,9},{8,10},{9,11},{10,... | collective-permute-start | bytes 1179656 | tf_op jit(solution)/shard_map/ppermute | solution.py:208
  42.4 8.2 %collective-permute-done.6.refs_2_ = bf16[768,256]{1,0:T(8,128)(2,1)} collective-permute-done((bf16[768,256]{1,0:T(8,128)(2,1)S(1)}, bf16[768,256]{1,0:T(8,128)(2,1)}, u32[]{:S(2)}, u32[]{:S(2)}) %collective-permute-start.6) | collective-permute-done | bytes 393248 | tf_op jit(solution)/shard_map/ppermute | solution.py:209
  53.9 12.7 %collective-permute-start.10 = (bf16[768,256]{1,0:T(8,128)(2,1)}, bf16[768,256]{1,0:T(8,128)(2,1)}, u32[]{:S(2)}, u32[]{:S(2)}) collective-permute-start(bf16[768,256]{1,0:T(8,128)(2,1)} %collective-permute-done.9.refs_1_), channel_id=1, source_target_pairs={{0,1},{1,0},{2,3},{3,2},{4,5},{5,4},{6,7},{7,6},{8,9},{9,8},{10,11... | collective-permute-start | bytes 1179656 | tf_op jit(solution)/shard_map/ppermute | solution.py:210
  66.8 4.1 %copy.29 = bf16[256,4096]{0,1:T(8,128)(2,1)} copy(bf16[256,4096]{1,0:T(8,128)(2,1)} %param.14) | data formatting | bytes 4194304 | tf_op args[4]
  71.0 4.1 %copy.30 = bf16[256,16,256]{2,0,1:T(8,128)(2,1)} copy(bf16[256,16,256]{0,2,1:T(8,128)(2,1)} %bitcast.9) | data formatting | bytes 4194304 | tf_op jit(solution)/shard_map/reshape | solution.py:416
  100.3 7.7 %collective-permute-done.17.refs_9_ = bf16[800,512]{1,0:T(8,128)(2,1)} collective-permute-done((bf16[800,512]{1,0:T(8,128)(2,1)S(1)}, bf16[800,512]{1,0:T(8,128)(2,1)}, u32[]{:S(2)}, u32[]{:S(2)}) %collective-permute-start.17) | collective-permute-done | bytes 819232 | tf_op jit(solution)/shard_map/ppermute | solution.py:221
  111.0 4.4 %collective-permute-done.15.refs_7_ = bf16[800,512]{1,0:T(8,128)(2,1)} collective-permute-done((bf16[800,512]{1,0:T(8,128)(2,1)S(1)}, bf16[800,512]{1,0:T(8,128)(2,1)}, u32[]{:S(2)}, u32[]{:S(2)}) %collective-permute-start.15) | collective-permute-done | bytes 819232 | tf_op jit(solution)/shard_map/ppermute | solution.py:219
  117.0 5.1 %all-to-all-start = ((bf16[16,256,256]{2,1,0:T(8,128)(2,1)}), bf16[16,256,256]{2,1,0:T(8,128)(2,1)S(1)}, u32[]{:S(2)}, u32[]{:S(2)}) async-start(bf16[16,256,256]{2,1,0:T(8,128)(2,1)} %bitcast.8), calls=%async_computation | async-start | bytes 4194304 | tf_op jit(solution)/shard_map/all_to_all | solution.py:419
  122.8 5.5 %collective-permute-done.19.refs_11_ = bf16[800,512]{1,0:T(8,128)(2,1)} collective-permute-done((bf16[800,512]{1,0:T(8,128)(2,1)}, bf16[800,512]{1,0:T(8,128)(2,1)}, u32[]{:S(2)}, u32[]{:S(2)}) %collective-permute-start.19) | collective-permute-done | bytes 819232 | tf_op jit(solution)/shard_map/ppermute | solution.py:220
  139.0 25.9 %collective-permute-done.20.refs_12_ = bf16[800,512]{1,0:T(8,128)(2,1)} collective-permute-done((bf16[800,512]{1,0:T(8,128)(2,1)}, bf16[800,512]{1,0:T(8,128)(2,1)}, u32[]{:S(2)}, u32[]{:S(2)}) %collective-permute-start.20) | collective-permute-done | bytes 819232 | tf_op jit(solution)/shard_map/ppermute | solution.py:221
  170.4 9.3 %collective-permute-done.21.refs_13_ = bf16[272,512]{1,0:T(8,128)(2,1)} collective-permute-done((bf16[272,512]{1,0:T(8,128)(2,1)}, bf16[272,512]{1,0:T(8,128)(2,1)}, u32[]{:S(2)}, u32[]{:S(2)}) %collective-permute-start.21) | collective-permute-done | bytes 278560 | tf_op jit(solution)/shard_map/ppermute | solution.py:219
  184.8 15.6 %attention.1.refs_1_ = bf16[768,256]{1,0:T(8,128)(2,1)S(1)} custom-call(s32[48]{0:T(128)S(1)} %get-tuple-element.18.refs_0_, s32[48]{0:T(128)S(1)} %get-tuple-element.17.refs_1_, s32[2]{0:T(128)S(1)} %copy-done.24, bf16[800,256]{1,0:T(8,128)(2,1)S(1)} %copy-done.4, s32[128,1]{1,0:T(8,128)S(1)} %copy.31.refs_4_, s32[1,32]{1,0:T(1,128)S(1)} %bitcast.7, ...), custom_call_target="tpu_custom_call" | custom-call | flops 2147483648 | bytes 14680064 | tf_op jit(solution)/shard_map/attention/pallas_call | solution.py:354
  200.4 3.9 %collective-permute-start.34 = (bf16[768,256]{1,0:T(8,128)(2,1)S(1)}, bf16[768,256]{1,0:T(8,128)(2,1)S(1)}, u32[]{:S(2)}, u32[]{:S(2)}) collective-permute-start(bf16[768,256]{1,0:T(8,128)(2,1)S(1)} %attention.1.refs_1_), channel_id=1, source_target_pairs={{0,2},{1,3},{2,4},{3,5},{4,6},{5,7},{6,8},{7,9},{8,10},{9,11},{10,... | collective-permute-start | bytes 1179656 | tf_op jit(solution)/shard_map/ppermute | solution.py:208
  204.3 8.9 %collective-permute-done.34.refs_1_ = bf16[768,256]{1,0:T(8,128)(2,1)S(1)} collective-permute-done((bf16[768,256]{1,0:T(8,128)(2,1)S(1)}, bf16[768,256]{1,0:T(8,128)(2,1)S(1)}, u32[]{:S(2)}, u32[]{:S(2)}) %collective-permute-start.34) | collective-permute-done | bytes 393248 | tf_op jit(solution)/shard_map/ppermute | solution.py:208
  213.2 3.7 %collective-permute-start.35 = (bf16[768,256]{1,0:T(8,128)(2,1)S(1)}, bf16[768,256]{1,0:T(8,128)(2,1)S(1)}, u32[]{:S(2)}, u32[]{:S(2)}) collective-permute-start(bf16[768,256]{1,0:T(8,128)(2,1)S(1)} %collective-permute-done.34.refs_1_), channel_id=1, source_target_pairs={{0,2},{1,3},{2,4},{3,5},{4,6},{5,7},{6,8},{7,9},{8,10},{9,11},{10,... | collective-permute-start | bytes 1179656 | tf_op jit(solution)/shard_map/ppermute | solution.py:208
  217.7 7.3 %collective-permute-done.35.refs_1_ = bf16[768,256]{1,0:T(8,128)(2,1)S(1)} collective-permute-done((bf16[768,256]{1,0:T(8,128)(2,1)S(1)}, bf16[768,256]{1,0:T(8,128)(2,1)S(1)}, u32[]{:S(2)}, u32[]{:S(2)}) %collective-permute-start.35) | collective-permute-done | bytes 393248 | tf_op jit(solution)/shard_map/ppermute | solution.py:208
  224.9 3.7 %collective-permute-start.42 = (bf16[768,256]{1,0:T(8,128)(2,1)S(1)}, bf16[768,256]{1,0:T(8,128)(2,1)S(1)}, u32[]{:S(2)}, u32[]{:S(2)}) collective-permute-start(bf16[768,256]{1,0:T(8,128)(2,1)S(1)} %collective-permute-done.35.refs_1_), channel_id=1, source_target_pairs={{0,2},{1,3},{2,4},{3,5},{4,6},{5,7},{6,8},{7,9},{8,10},{9,11},{10,... | collective-permute-start | bytes 1179656 | tf_op jit(solution)/shard_map/ppermute | solution.py:208
  235.8 3.7 %collective-permute-start.43 = (bf16[768,256]{1,0:T(8,128)(2,1)S(1)}, bf16[768,256]{1,0:T(8,128)(2,1)}, u32[]{:S(2)}, u32[]{:S(2)}) collective-permute-start(bf16[768,256]{1,0:T(8,128)(2,1)S(1)} %collective-permute-done.42.refs_1_), channel_id=1, source_target_pairs={{0,2},{1,3},{2,4},{3,5},{4,6},{5,7},{6,8},{7,9},{8,10},{9,11},{10,... | collective-permute-start | bytes 1179656 | tf_op jit(solution)/shard_map/ppermute | solution.py:208
  243.0 8.4 %collective-permute-done.40.refs_2_ = bf16[768,256]{1,0:T(8,128)(2,1)} collective-permute-done((bf16[768,256]{1,0:T(8,128)(2,1)S(1)}, bf16[768,256]{1,0:T(8,128)(2,1)}, u32[]{:S(2)}, u32[]{:S(2)}) %collective-permute-start.40) | collective-permute-done | bytes 393248 | tf_op jit(solution)/shard_map/ppermute | solution.py:209
  (164 shorter events, 96.4 us)
Async XLA Ops:
  28.9 21.8 %collective-permute-start.2 = (bf16[768,256]{1,0:T(8,128)(2,1)S(1)}, bf16[768,256]{1,0:T(8,128)(2,1)}, u32[]{:S(2)}, u32[]{:S(2)}) collective-permute-start(bf16[768,256]{1,0:T(8,128)(2,1)S(1)} %collective-permute-done.1.refs_1_), channel_id=1, source_target_pairs={{0,1},{1,0},{2,3},{3,2},{4,5},{5,4},{6,7},{7,6},{8,9},{9,8},{10,11... | collective-permute-start | bytes 1179656 | tf_op jit(solution)/shard_map/ppermute | solution.py:210
  29.5 21.2 %collective-permute-start.6 = (bf16[768,256]{1,0:T(8,128)(2,1)S(1)}, bf16[768,256]{1,0:T(8,128)(2,1)}, u32[]{:S(2)}, u32[]{:S(2)}) collective-permute-start(bf16[768,256]{1,0:T(8,128)(2,1)S(1)} %collective-permute-done.5.refs_3_), channel_id=1, source_target_pairs={{0,14},{1,15},{2,0},{3,1},{4,2},{5,3},{6,4},{7,5},{8,6},{9,7},{10,... | collective-permute-start | bytes 1179656 | tf_op jit(solution)/shard_map/ppermute | solution.py:209
  33.2 20.7 %collective-permute-start.9 = (bf16[768,256]{1,0:T(8,128)(2,1)S(1)}, bf16[768,256]{1,0:T(8,128)(2,1)}, u32[]{:S(2)}, u32[]{:S(2)}) collective-permute-start(bf16[768,256]{1,0:T(8,128)(2,1)S(1)} %collective-permute-done.8.refs_1_), channel_id=1, source_target_pairs={{0,2},{1,3},{2,4},{3,5},{4,6},{5,7},{6,8},{7,9},{8,10},{9,11},{10,... | collective-permute-start | bytes 1179656 | tf_op jit(solution)/shard_map/ppermute | solution.py:208
  38.9 42.3 %collective-permute-start.13 = (bf16[768,256]{1,0:T(8,128)(2,1)S(1)}, bf16[768,256]{1,0:T(8,128)(2,1)}, u32[]{:S(2)}, u32[]{:S(2)}) collective-permute-start(bf16[768,256]{1,0:T(8,128)(2,1)S(1)} %collective-permute-done.refs_1_), channel_id=1, source_target_pairs={{0,1},{1,0},{2,3},{3,2},{4,5},{5,4},{6,7},{7,6},{8,9},{9,8},{10,11... | collective-permute-start | bytes 1179656 | tf_op jit(solution)/shard_map/ppermute | solution.py:210
  42.2 41.9 %collective-permute-start.12 = (bf16[768,256]{1,0:T(8,128)(2,1)}, bf16[768,256]{1,0:T(8,128)(2,1)}, u32[]{:S(2)}, u32[]{:S(2)}) collective-permute-start(bf16[768,256]{1,0:T(8,128)(2,1)} %collective-permute-done.11.refs_2_), channel_id=1, source_target_pairs={{0,14},{1,15},{2,0},{3,1},{4,2},{5,3},{6,4},{7,5},{8,6},{9,7},{10,... | collective-permute-start | bytes 1179656 | tf_op jit(solution)/shard_map/ppermute | solution.py:209
  50.6 39.4 %collective-permute-start.7 = (bf16[768,256]{1,0:T(8,128)(2,1)}, bf16[768,256]{1,0:T(8,128)(2,1)}, u32[]{:S(2)}, u32[]{:S(2)}) collective-permute-start(bf16[768,256]{1,0:T(8,128)(2,1)} %collective-permute-done.6.refs_2_), channel_id=1, source_target_pairs={{0,14},{1,15},{2,0},{3,1},{4,2},{5,3},{6,4},{7,5},{8,6},{9,7},{10,... | collective-permute-start | bytes 1179656 | tf_op jit(solution)/shard_map/ppermute | solution.py:209
  50.6 39.4 %collective-permute-start.3 = (bf16[768,256]{1,0:T(8,128)(2,1)}, bf16[768,256]{1,0:T(8,128)(2,1)}, u32[]{:S(2)}, u32[]{:S(2)}) collective-permute-start(bf16[768,256]{1,0:T(8,128)(2,1)} %collective-permute-done.2.refs_3_), channel_id=1, source_target_pairs={{0,2},{1,3},{2,4},{3,5},{4,6},{5,7},{6,8},{7,9},{8,10},{9,11},{10,... | collective-permute-start | bytes 1179656 | tf_op jit(solution)/shard_map/ppermute | solution.py:208
  53.9 36.2 %collective-permute-start.10 = (bf16[768,256]{1,0:T(8,128)(2,1)}, bf16[768,256]{1,0:T(8,128)(2,1)}, u32[]{:S(2)}, u32[]{:S(2)}) collective-permute-start(bf16[768,256]{1,0:T(8,128)(2,1)} %collective-permute-done.9.refs_1_), channel_id=1, source_target_pairs={{0,1},{1,0},{2,3},{3,2},{4,5},{5,4},{6,7},{7,6},{8,9},{9,8},{10,11... | collective-permute-start | bytes 1179656 | tf_op jit(solution)/shard_map/ppermute | solution.py:210
  97.0 18.4 %collective-permute-start.15 = (bf16[800,512]{1,0:T(8,128)(2,1)S(1)}, bf16[800,512]{1,0:T(8,128)(2,1)}, u32[]{:S(2)}, u32[]{:S(2)}) collective-permute-start(bf16[800,512]{1,0:T(8,128)(2,1)S(1)} %get-tuple-element.11.refs_6_), channel_id=1, source_target_pairs={{0,32},{16,48},{32,64},{48,80},{64,96},{80,112},{96,0},{112,16},{1... | collective-permute-start | bytes 2457608 | tf_op jit(solution)/shard_map/ppermute | solution.py:219
  98.6 24.1 %collective-permute-start.16 = (bf16[800,512]{1,0:T(8,128)(2,1)S(1)}, bf16[800,512]{1,0:T(8,128)(2,1)}, u32[]{:S(2)}, u32[]{:S(2)}) collective-permute-start(bf16[800,512]{1,0:T(8,128)(2,1)S(1)} %get-tuple-element.11.refs_6_), channel_id=1, source_target_pairs={{0,96},{16,112},{32,0},{48,16},{64,32},{80,48},{96,64},{112,80},{1... | collective-permute-start | bytes 2457608 | tf_op jit(solution)/shard_map/ppermute | solution.py:220
  107.9 20.3 %collective-permute-start.19 = (bf16[800,512]{1,0:T(8,128)(2,1)}, bf16[800,512]{1,0:T(8,128)(2,1)}, u32[]{:S(2)}, u32[]{:S(2)}) collective-permute-start(bf16[800,512]{1,0:T(8,128)(2,1)} %collective-permute-done.17.refs_9_), channel_id=1, source_target_pairs={{0,96},{16,112},{32,0},{48,16},{64,32},{80,48},{96,64},{112,80},{1... | collective-permute-start | bytes 2457608 | tf_op jit(solution)/shard_map/ppermute | solution.py:220
  117.0 138.8 %all-to-all-start = ((bf16[16,256,256]{2,1,0:T(8,128)(2,1)}), bf16[16,256,256]{2,1,0:T(8,128)(2,1)S(1)}, u32[]{:S(2)}, u32[]{:S(2)}) async-start(bf16[16,256,256]{2,1,0:T(8,128)(2,1)} %bitcast.8), calls=%async_computation | async-start | bytes 4194304 | tf_op jit(solution)/shard_map/all_to_all | solution.py:419
  122.7 15.8 %collective-permute-start.26 = (bf16[800,512]{1,0:T(8,128)(2,1)}, bf16[800,512]{1,0:T(8,128)(2,1)}, u32[]{:S(2)}, u32[]{:S(2)}) collective-permute-start(bf16[800,512]{1,0:T(8,128)(2,1)} %collective-permute-done.16.refs_8_), channel_id=1, source_target_pairs={{0,16},{16,0},{32,48},{48,32},{64,80},{80,64},{96,112},{112,96},{1... | collective-permute-start | bytes 2457608 | tf_op jit(solution)/shard_map/ppermute | solution.py:239
  129.3 35.6 %collective-permute-start.20 = (bf16[800,512]{1,0:T(8,128)(2,1)}, bf16[800,512]{1,0:T(8,128)(2,1)}, u32[]{:S(2)}, u32[]{:S(2)}) collective-permute-start(bf16[800,512]{1,0:T(8,128)(2,1)} %collective-permute-done.15.refs_7_), channel_id=1, source_target_pairs={{0,128},{16,144},{32,160},{48,176},{64,192},{80,208},{96,224},{112... | collective-permute-start | bytes 2457608 | tf_op jit(solution)/shard_map/ppermute | solution.py:221
  132.6 37.6 %collective-permute-start.22 = (bf16[272,512]{1,0:T(8,128)(2,1)}, bf16[272,512]{1,0:T(8,128)(2,1)S(1)}, u32[]{:S(2)}, u32[]{:S(2)}) collective-permute-start(bf16[272,512]{1,0:T(8,128)(2,1)} %slice.13), channel_id=1, source_target_pairs={{0,96},{16,112},{32,0},{48,16},{64,32},{80,48},{96,64},{112,80},{1... | collective-permute-start | bytes 835592 | tf_op jit(solution)/shard_map/ppermute | solution.py:220
  135.3 33.9 %collective-permute-start.23 = (bf16[256,512]{1,0:T(8,128)(2,1)}, bf16[256,512]{1,0:T(8,128)(2,1)}, u32[]{:S(2)}, u32[]{:S(2)}) collective-permute-start(bf16[256,512]{1,0:T(8,128)(2,1)} %slice.14), channel_id=1, source_target_pairs={{0,128},{16,144},{32,160},{48,176},{64,192},{80,208},{96,224},{112... | collective-permute-start | bytes 786440 | tf_op jit(solution)/shard_map/ppermute | solution.py:221
  138.5 44.3 %collective-permute-start.29 = (bf16[800,512]{1,0:T(8,128)(2,1)}, bf16[800,512]{1,0:T(8,128)(2,1)}, u32[]{:S(2)}, u32[]{:S(2)}) collective-permute-start(bf16[800,512]{1,0:T(8,128)(2,1)} %collective-permute-done.19.refs_11_), channel_id=1, source_target_pairs={{0,16},{16,0},{32,48},{48,32},{64,80},{80,64},{96,112},{112,96},{1... | collective-permute-start | bytes 2457608 | tf_op jit(solution)/shard_map/ppermute | solution.py:239
  138.5 44.3 %collective-permute-start.28 = (bf16[800,512]{1,0:T(8,128)(2,1)}, bf16[800,512]{1,0:T(8,128)(2,1)}, u32[]{:S(2)}, u32[]{:S(2)}) collective-permute-start(bf16[800,512]{1,0:T(8,128)(2,1)} %collective-permute-done.18.refs_10_), channel_id=1, source_target_pairs={{0,16},{16,0},{32,48},{48,32},{64,80},{80,64},{96,112},{112,96},{1... | collective-permute-start | bytes 2457608 | tf_op jit(solution)/shard_map/ppermute | solution.py:239
  164.9 17.9 %collective-permute-start.30 = (bf16[800,512]{1,0:T(8,128)(2,1)}, bf16[800,512]{1,0:T(8,128)(2,1)}, u32[]{:S(2)}, u32[]{:S(2)}) collective-permute-start(bf16[800,512]{1,0:T(8,128)(2,1)} %collective-permute-done.20.refs_12_), channel_id=1, source_target_pairs={{0,16},{16,0},{32,48},{48,32},{64,80},{80,64},{96,112},{112,96},{1... | collective-permute-start | bytes 2457608 | tf_op jit(solution)/shard_map/ppermute | solution.py:239
  230.4 21.0 %collective-permute-start.40 = (bf16[768,256]{1,0:T(8,128)(2,1)S(1)}, bf16[768,256]{1,0:T(8,128)(2,1)}, u32[]{:S(2)}, u32[]{:S(2)}) collective-permute-start(bf16[768,256]{1,0:T(8,128)(2,1)S(1)} %collective-permute-done.39.refs_3_), channel_id=1, source_target_pairs={{0,14},{1,15},{2,0},{3,1},{4,2},{5,3},{6,4},{7,5},{8,6},{9,7},{10,... | collective-permute-start | bytes 1179656 | tf_op jit(solution)/shard_map/ppermute | solution.py:209
  230.4 21.0 %collective-permute-start.36 = (bf16[768,256]{1,0:T(8,128)(2,1)S(1)}, bf16[768,256]{1,0:T(8,128)(2,1)}, u32[]{:S(2)}, u32[]{:S(2)}) collective-permute-start(bf16[768,256]{1,0:T(8,128)(2,1)S(1)} %collective-permute-done.35.refs_1_), channel_id=1, source_target_pairs={{0,1},{1,0},{2,3},{3,2},{4,5},{5,4},{6,7},{7,6},{8,9},{9,8},{10,11... | collective-permute-start | bytes 1179656 | tf_op jit(solution)/shard_map/ppermute | solution.py:210
  235.8 18.8 %collective-permute-start.43 = (bf16[768,256]{1,0:T(8,128)(2,1)S(1)}, bf16[768,256]{1,0:T(8,128)(2,1)}, u32[]{:S(2)}, u32[]{:S(2)}) collective-permute-start(bf16[768,256]{1,0:T(8,128)(2,1)S(1)} %collective-permute-done.42.refs_1_), channel_id=1, source_target_pairs={{0,2},{1,3},{2,4},{3,5},{4,6},{5,7},{6,8},{7,9},{8,10},{9,11},{10,... | collective-permute-start | bytes 1179656 | tf_op jit(solution)/shard_map/ppermute | solution.py:208
  241.4 16.7 %collective-permute-start.47 = (bf16[768,256]{1,0:T(8,128)(2,1)S(1)}, bf16[768,256]{1,0:T(8,128)(2,1)}, u32[]{:S(2)}, u32[]{:S(2)}) collective-permute-start(bf16[768,256]{1,0:T(8,128)(2,1)S(1)} %collective-permute-done.34.refs_1_), channel_id=1, source_target_pairs={{0,1},{1,0},{2,3},{3,2},{4,5},{5,4},{6,7},{7,6},{8,9},{9,8},{10,11... | collective-permute-start | bytes 1179656 | tf_op jit(solution)/shard_map/ppermute | solution.py:210
  243.0 17.4 %collective-permute-start.46 = (bf16[768,256]{1,0:T(8,128)(2,1)}, bf16[768,256]{1,0:T(8,128)(2,1)}, u32[]{:S(2)}, u32[]{:S(2)}) collective-permute-start(bf16[768,256]{1,0:T(8,128)(2,1)} %collective-permute-done.45.refs_2_), channel_id=1, source_target_pairs={{0,14},{1,15},{2,0},{3,1},{4,2},{5,3},{6,4},{7,5},{8,6},{9,7},{10,... | collective-permute-start | bytes 1179656 | tf_op jit(solution)/shard_map/ppermute | solution.py:209
  (52 other events, 634.4 us)
